TPU v7x, 32 devices: a whole 2x2x4 slice. The times are simulated.
32 devices in a mesh: gx: 8 (over z, y), gy: 4 (over x, core).
Axes of the slice: x: 2, y: 2, z: 4, core: 2. Of those that a mesh axis runs over, the one named last changes fastest.
Arguments:
- point_feats: bfloat16 [32, 262144], P(None, ('gx', 'gy')), may hold values from -1 to 1
- point_targets: bfloat16 [262144], P(('gx', 'gy')), may hold values from -6 to 6
- point_lists: int32 [32768, 8], P(('gx', 'gy')), may hold values from -1 to 8191, as said below
- brick_adjacency: int32 [1024, 4], P(('gx', 'gy')), may hold values from -1 to 1023, as said below
- voxel_feats: float32 [1024, 32, 512], P(('gx', 'gy')), may hold values from -0.25 to 0.25
- voxel_reg: float32 [1024, 512], P(('gx', 'gy')), may hold values from 0.25 to 2
Outputs:
- solution: float32 [1024, 512], P(('gx', 'gy'))
- residual: float32 [1024, 512], P(('gx', 'gy'))
Inputs may be any that keep to these rules, and one draw needn't show every extreme that they name: `point_lists`: row s * 1024 + b lists, in its first slots, distinct indices of the points of source device s in brick b, all within that device's rows b * 8 to b * 8 + 7, then -1 in the remaining slots. Point rows named by no list are unused. `brick_adjacency`: entry k of brick b is the lattice neighbour of b in direction k (minus along the road, plus along the road, minus across, plus across) or -1; the relation is symmetric and -1 wherever the neighbour lies outside the lattice.
All inputs are finite; a program needn't handle non-finite values.
Results may differ from a plain program's by a relative error of at most 0.0003.
Values may be sent and summed in bfloat16 or wider, within the bound.
A program may use at most 64 MiB of HBM per device.

v0:
```python
import jax
import jax.numpy as jnp
from jax import lax
from jax.sharding import PartitionSpec as P

BX = 8
BY = 4
ITERS = 3


coupling_weight = 1.0


def extended(block, sides, width):
    for axis, dim in sides:
        count = lax.axis_size(axis)
        forward = [(i, i + 1) for i in range(count - 1)]
        backward = [(target, source) for source, target in forward]
        low = lax.ppermute(
            lax.slice_in_dim(block, block.shape[dim] - width, None, axis=dim), axis, forward
        )
        high = lax.ppermute(lax.slice_in_dim(block, 0, width, axis=dim), axis, backward)
        block = jnp.concatenate([low, block, high], axis=dim)
    return block


def neighbour_sum(padded, mask):
    total = mask[..., 0:1] * padded[:-2, 1:-1] + mask[..., 1:2] * padded[2:, 1:-1]
    return total + mask[..., 2:3] * padded[1:-1, :-2] + mask[..., 3:4] * padded[1:-1, 2:]


def shards(point_feats, point_targets, point_lists, brick_adjacency, voxel_feats, voxel_reg):
    feat_count = point_feats.shape[0]
    brick_total, slots = point_lists.shape
    local_bricks = voxel_feats.shape[0]
    devices = brick_total // local_bricks
    live = point_lists >= 0
    offset = point_lists - jnp.arange(brick_total, dtype=jnp.int32)[:, None] * slots
    choose = (offset[:, :, None] == jnp.arange(slots, dtype=jnp.int32)[None, None, :]) & live[
        :, :, None
    ]
    choose = choose.astype(jnp.bfloat16)
    blocks = point_feats.reshape(feat_count, brick_total, slots)
    picked = jnp.einsum("ibd,bcd->ibc", blocks, choose, preferred_element_type=jnp.float32).astype(
        jnp.bfloat16
    )
    target_blocks = point_targets.reshape(brick_total, slots)
    targets = jnp.einsum(
        "bd,bcd->bc", target_blocks, choose, preferred_element_type=jnp.float32
    ).astype(jnp.bfloat16)
    sending = picked.reshape(feat_count, devices, local_bricks * slots)
    target_rows = targets.reshape(1, devices, local_bricks * slots)
    got_feats, got_targets = (
        lax.all_to_all(sending, ("gx", "gy"), split_axis=1, concat_axis=1, tiled=True),
        lax.all_to_all(target_rows, ("gx", "gy"), split_axis=1, concat_axis=1, tiled=True),
    )
    got_feats = got_feats.reshape(feat_count, devices, local_bricks, slots)
    got_targets = got_targets.reshape(devices, local_bricks, slots)
    moments = jnp.einsum("isbc,jsbc->bij", got_feats, got_feats, preferred_element_type=jnp.float32)
    gathered = jnp.einsum(
        "sbc,isbc->bi", got_targets, got_feats, preferred_element_type=jnp.float32
    )
    mask = (brick_adjacency >= 0).astype(jnp.float32).reshape(BX, BY, 4)
    degree = jnp.sum(mask, axis=-1, keepdims=True)

    def operate(vector):
        projected = jnp.einsum("bik,bk->bi", voxel_feats, vector, precision=lax.Precision.HIGHEST)
        lattice = projected.reshape(BX, BY, feat_count)
        padded = extended(lattice, (("gx", 0), ("gy", 1)), 1)
        coupled = (degree * lattice - neighbour_sum(padded, mask)).reshape(local_bricks, feat_count)
        middle = jnp.einsum("bij,bj->bi", moments, projected, precision=lax.Precision.HIGHEST)
        middle = middle + coupling_weight * coupled
        back = jnp.einsum("bik,bi->bk", voxel_feats, middle, precision=lax.Precision.HIGHEST)
        return back + voxel_reg * vector

    def two_products(values, image):
        return lax.psum((jnp.sum(values * values), jnp.sum(values * image)), ("gx", "gy"))

    rhs = jnp.einsum("bik,bi->bk", voxel_feats, gathered, precision=lax.Precision.HIGHEST)
    solution = jnp.zeros_like(rhs)
    residual = rhs
    image = operate(residual)
    norm_now, product = two_products(residual, image)
    alpha = norm_now / product
    direction, carried = (residual, image)
    for iteration in range(ITERS):
        solution = solution + alpha * direction
        residual = residual - alpha * carried
        if iteration + 1 < ITERS:
            image = operate(residual)
            norm_next, product = two_products(residual, image)
            ratio = norm_next / norm_now
            alpha = norm_next / (product - ratio * norm_next / alpha)
            direction = residual + ratio * direction
            carried = image + ratio * carried
            norm_now = norm_next
    return (solution, residual)


def solution(mesh):
    placed = (
        P(None, ("gx", "gy")),
        P(("gx", "gy")),
        P(("gx", "gy"), None),
        P(("gx", "gy"), None),
        P(("gx", "gy"), None, None),
        P(("gx", "gy"), None),
    )
    return jax.shard_map(
        shards,
        mesh=mesh,
        in_specs=placed,
        out_specs=(P(("gx", "gy"), None), P(("gx", "gy"), None)),
        check_vma=False,
    )
```

profile of v0, /device:TPU:0, one launch (start us, length us, event | category | flops | bytes accessed | tf_op | source)
XLA Modules:
  0.0 251.1 jit_solution(11795975120160489143)
XLA Ops:
  2.8 2.1 reshape.98
  4.9 5.8 %fusion.3 = f32[1024,1,8]{2,1,0:T(1,128)S(1)} fusion(bf16[1024,8,1]{1,2,0:T(2,128)(2,1)} %reshape.98, s32[1024,8]{1,0:T(8,128)S(1)} %copy.33, pred[1024,8]{1,0:T(8,128)(4,1)S(1)} %copy.34), kind=kOutput, calls=%fused_computation.3 | convolution fusion | flops 262144 | bytes 90112 | tf_op jit(solution)/shard_map/bd,bcd->bc/dot_general | solution.py:48
  12.9 7.3 %all-to-all-start = ((bf16[32,2,128]{2,1,0:T(2,128)(2,1)}), bf16[32,2,128]{2,1,0:T(2,128)(2,1)S(1)}, u32[]{:S(2)}, u32[]{:S(2)}) async-start(bf16[32,2,128]{2,1,0:T(2,128)(2,1)} %reshape.100), calls=%async_computation | async-start | bytes 32768 | tf_op jit(solution)/shard_map/all_to_all | solution.py:55
  20.3 1.8 copy.37
  22.1 7.1 %fusion.10 = bf16[1024,8,32]{2,1,0:T(8,128)(2,1)} fusion(bf16[32,8192]{0,1:T(8,128)(2,1)} %copy.37, s32[1024,8]{1,0:T(8,128)S(1)} %copy.33, pred[1024,8]{1,0:T(8,128)(4,1)S(1)} %copy-done.5), kind=kOutput, calls=%fused_computation.9 | convolution fusion | flops 4587520 | bytes 1089536 | tf_op jit(solution)/shard_map/ibd,bcd->ibc/dot_general | solution.py:44
  29.2 2.6 %copy.38 = bf16[32,32,256]{2,0,1:T(8,128)(2,1)} copy(bf16[32,32,256]{0,2,1:T(8,128)(2,1)} %bitcast.158) | data formatting | bytes 1048576 | tf_op jit(solution)/shard_map/reshape | solution.py:51
  31.8 5.8 %all-to-all-start.1 = ((bf16[32,32,256]{2,0,1:T(8,128)(2,1)}), bf16[32,32,256]{2,0,1:T(8,128)(2,1)S(1)}, u32[]{:S(2)}, u32[]{:S(2)}) async-start(bf16[32,32,256]{2,0,1:T(8,128)(2,1)} %copy.38), calls=%async_computation.1 | async-start | bytes 1048576 | tf_op jit(solution)/shard_map/all_to_all | solution.py:54
  38.0 15.3 %all-to-all-done.1 = bf16[32,32,256]{2,0,1:T(8,128)(2,1)S(1)} async-done(((bf16[32,32,256]{2,0,1:T(8,128)(2,1)}), bf16[32,32,256]{2,0,1:T(8,128)(2,1)S(1)}, u32[]{:S(2)}, u32[]{:S(2)}) %all-to-all-start.1) | async-done | bytes 524320 | tf_op jit(solution)/shard_map/all_to_all | solution.py:54
  53.2 3.9 %copy.39 = bf16[32,32,256]{1,0,2:T(8,128)(2,1)} copy(bf16[32,32,256]{2,0,1:T(8,128)(2,1)S(1)} %all-to-all-done.1) | data formatting | bytes 1048576 | tf_op jit(solution)/shard_map/all_to_all | solution.py:54
  57.2 2.2 convolution_bitcast_fusion.1
  60.5 1.8 fusion.25
  62.4 3.1 %collective-permute-start = (f32[1,4,32]{2,1,0:T(4,128)S(1)}, f32[1,4,32]{2,1,0:T(4,128)S(1)}, u32[]{:S(2)}, u32[]{:S(2)}) collective-permute-start(f32[1,4,32]{2,1,0:T(4,128)S(1)} %get-tuple-element.31), channel_id=1, source_target_pairs={{0,4},{4,8},{8,12},{12,16},{16,20},{20,24},{24,28},{1,5},{5,9},{9,... | collective-permute-start | bytes 1544 | tf_op jit(solution)/shard_map/ppermute | solution.py:19
  67.5 3.5 %collective-permute-done.1 = f32[1,4,32]{2,1,0:T(4,128)S(1)} collective-permute-done((f32[1,4,32]{2,1,0:T(4,128)S(1)}, f32[1,4,32]{2,1,0:T(4,128)S(1)}, u32[]{:S(2)}, u32[]{:S(2)}) %collective-permute-start.1) | collective-permute-done | bytes 544 | tf_op jit(solution)/shard_map/ppermute | solution.py:22
  74.5 2.2 collective-permute-done.3
  78.6 40.8 %all-reduce.2 = (f32[]{:T(128)}, f32[]{:T(128)}) all-reduce(f32[]{:T(128)} %get-tuple-element.7, f32[]{:T(128)} %get-tuple-element.6), channel_id=1, replica_groups=mesh['gx'=8,'gy'=4] {'gx','gy'}, use_global_device_ids=true, to_apply=%region_1.0 | all-reduce | flops 2 | bytes 16 | tf_op jit(solution)/shard_map/psum | solution.py:77
  120.7 1.8 fusion.23
  122.5 4.4 %collective-permute-start.4 = (f32[1,4,32]{2,1,0:T(4,128)S(1)}, f32[1,4,32]{2,1,0:T(4,128)S(1)}, u32[]{:S(2)}, u32[]{:S(2)}) collective-permute-start(f32[1,4,32]{2,1,0:T(4,128)S(1)} %get-tuple-element.25), channel_id=1, source_target_pairs={{0,4},{4,8},{8,12},{12,16},{16,20},{20,24},{24,28},{1,5},{5,9},{9,... | collective-permute-start | bytes 1544 | tf_op jit(solution)/shard_map/ppermute | solution.py:19
  128.2 4.2 %collective-permute-done.5 = f32[1,4,32]{2,1,0:T(4,128)S(1)} collective-permute-done((f32[1,4,32]{2,1,0:T(4,128)S(1)}, f32[1,4,32]{2,1,0:T(4,128)S(1)}, u32[]{:S(2)}, u32[]{:S(2)}) %collective-permute-start.5) | collective-permute-done | bytes 544 | tf_op jit(solution)/shard_map/ppermute | solution.py:22
  139.2 41.8 %all-reduce.1 = (f32[]{:T(128)}, f32[]{:T(128)}) all-reduce(f32[]{:T(128)} %get-tuple-element.5, f32[]{:T(128)} %get-tuple-element.4), channel_id=1, replica_groups=mesh['gx'=8,'gy'=4] {'gx','gy'}, use_global_device_ids=true, to_apply=%region_6.0 | all-reduce | flops 2 | bytes 16 | tf_op jit(solution)/shard_map/psum | solution.py:77
  185.7 1.8 fusion.21
  187.5 4.4 %collective-permute-start.8 = (f32[1,4,32]{2,1,0:T(4,128)S(1)}, f32[1,4,32]{2,1,0:T(4,128)S(1)}, u32[]{:S(2)}, u32[]{:S(2)}) collective-permute-start(f32[1,4,32]{2,1,0:T(4,128)S(1)} %get-tuple-element.23), channel_id=1, source_target_pairs={{0,4},{4,8},{8,12},{12,16},{16,20},{20,24},{24,28},{1,5},{5,9},{9,... | collective-permute-start | bytes 1544 | tf_op jit(solution)/shard_map/ppermute | solution.py:19
  193.3 4.2 %collective-permute-done.9 = f32[1,4,32]{2,1,0:T(4,128)S(1)} collective-permute-done((f32[1,4,32]{2,1,0:T(4,128)S(1)}, f32[1,4,32]{2,1,0:T(4,128)S(1)}, u32[]{:S(2)}, u32[]{:S(2)}) %collective-permute-start.9) | collective-permute-done | bytes 544 | tf_op jit(solution)/shard_map/ppermute | solution.py:22
  201.0 1.6 collective-permute-done.11
  204.5 41.9 %all-reduce = (f32[]{:T(128)}, f32[]{:T(128)}) all-reduce(f32[]{:T(128)} %get-tuple-element.3, f32[]{:T(128)} %get-tuple-element.2), channel_id=1, replica_groups=mesh['gx'=8,'gy'=4] {'gx','gy'}, use_global_device_ids=true, to_apply=%region_10.0 | all-reduce | flops 2 | bytes 16 | tf_op jit(solution)/shard_map/psum | solution.py:77
  (75 shorter events, 28.7 us)
Async XLA Ops:
  0.6 58.8 %copy-start = (f32[32,32,512]{2,1,0:T(8,128)S(1)}, f32[32,32,512]{2,1,0:T(8,128)}, u32[]{:S(2)}) copy-start(f32[32,32,512]{2,1,0:T(8,128)} %param.10) | copy-start | bytes 6291460
  2.8 8.0 %copy-start.4 = (pred[1024,8]{1,0:T(8,128)(4,1)}, pred[1024,8]{1,0:T(8,128)(4,1)S(1)}, u32[]{:S(2)}) copy-start(pred[1024,8]{1,0:T(8,128)(4,1)S(1)} %copy.34) | copy-start | bytes 24580
  4.9 15.4 %copy-start.3 = (bf16[32,8192]{1,0:T(8,128)(2,1)S(1)}, bf16[32,8192]{1,0:T(8,128)(2,1)}, u32[]{:S(2)}) copy-start(bf16[32,8192]{1,0:T(8,128)(2,1)} %param.6) | copy-start | bytes 1572868
  11.1 11.0 %copy-start.5 = (pred[1024,8]{1,0:T(8,128)(4,1)S(1)}, pred[1024,8]{1,0:T(8,128)(4,1)}, u32[]{:S(2)}) copy-start(pred[1024,8]{1,0:T(8,128)(4,1)} %copy-done.4) | copy-start | bytes 24580
  12.9 18.8 %all-to-all-start = ((bf16[32,2,128]{2,1,0:T(2,128)(2,1)}), bf16[32,2,128]{2,1,0:T(2,128)(2,1)S(1)}, u32[]{:S(2)}, u32[]{:S(2)}) async-start(bf16[32,2,128]{2,1,0:T(2,128)(2,1)} %reshape.100), calls=%async_computation | async-start | bytes 32768 | tf_op jit(solution)/shard_map/all_to_all | solution.py:55
  29.2 8.4 %copy-start.6 = (s32[32,4]{0,1:T(4,128)S(1)}, s32[32,4]{0,1:T(4,128)}, u32[]{:S(2)}) copy-start(s32[32,4]{0,1:T(4,128)} %param.9) | copy-start | bytes 1540
  31.8 21.5 %all-to-all-start.1 = ((bf16[32,32,256]{2,0,1:T(8,128)(2,1)}), bf16[32,32,256]{2,0,1:T(8,128)(2,1)S(1)}, u32[]{:S(2)}, u32[]{:S(2)}) async-start(bf16[32,32,256]{2,0,1:T(8,128)(2,1)} %copy.38), calls=%async_computation.1 | async-start | bytes 1048576 | tf_op jit(solution)/shard_map/all_to_all | solution.py:54
  59.4 7.4 %copy-start.1 = (bf16[32,32,256]{1,0,2:T(8,128)(2,1)S(1)}, bf16[32,32,256]{1,0,2:T(8,128)(2,1)}, u32[]{:S(2)}) copy-start(bf16[32,32,256]{1,0,2:T(8,128)(2,1)} %copy.39) | copy-start | bytes 1572868
  62.4 5.1 %collective-permute-start = (f32[1,4,32]{2,1,0:T(4,128)S(1)}, f32[1,4,32]{2,1,0:T(4,128)S(1)}, u32[]{:S(2)}, u32[]{:S(2)}) collective-permute-start(f32[1,4,32]{2,1,0:T(4,128)S(1)} %get-tuple-element.31), channel_id=1, source_target_pairs={{0,4},{4,8},{8,12},{12,16},{16,20},{20,24},{24,28},{1,5},{5,9},{9,... | collective-permute-start | bytes 1544 | tf_op jit(solution)/shard_map/ppermute | solution.py:19
  65.5 5.5 %collective-permute-start.1 = (f32[1,4,32]{2,1,0:T(4,128)S(1)}, f32[1,4,32]{2,1,0:T(4,128)S(1)}, u32[]{:S(2)}, u32[]{:S(2)}) collective-permute-start(f32[1,4,32]{2,1,0:T(4,128)S(1)} %get-tuple-element.32), channel_id=1, source_target_pairs={{4,0},{8,4},{12,8},{16,12},{20,16},{24,20},{28,24},{5,1},{9,5},{13... | collective-permute-start | bytes 1544 | tf_op jit(solution)/shard_map/ppermute | solution.py:22
  67.4 10.5 %copy-start.2 = (f32[32,512]{1,0:T(8,128)S(1)}, f32[32,512]{1,0:T(8,128)}, u32[]{:S(2)}) copy-start(f32[32,512]{1,0:T(8,128)} %param.11) | copy-start | bytes 196612
  71.0 3.5 %collective-permute-start.2 = (f32[10,1,32]{2,1,0:T(1,128)S(1)}, f32[10,1,32]{2,1,0:T(1,128)S(1)}, u32[]{:S(2)}, u32[]{:S(2)}) collective-permute-start(f32[10,1,32]{2,1,0:T(1,128)S(1)} %get-tuple-element.21), channel_id=1, source_target_pairs={{0,1},{1,2},{2,3},{4,5},{5,6},{6,7},{8,9},{9,10},{10,11},{12,13},{... | collective-permute-start | bytes 3848 | tf_op jit(solution)/shard_map/ppermute | solution.py:19
  72.3 4.4 %collective-permute-start.3 = (f32[10,1,32]{2,1,0:T(1,128)S(1)}, f32[10,1,32]{2,1,0:T(1,128)S(1)}, u32[]{:S(2)}, u32[]{:S(2)}) collective-permute-start(f32[10,1,32]{2,1,0:T(1,128)S(1)} %get-tuple-element.22), channel_id=1, source_target_pairs={{1,0},{2,1},{3,2},{5,4},{6,5},{7,6},{9,8},{10,9},{11,10},{13,12},{... | collective-permute-start | bytes 3848 | tf_op jit(solution)/shard_map/ppermute | solution.py:22
  122.5 5.7 %collective-permute-start.4 = (f32[1,4,32]{2,1,0:T(4,128)S(1)}, f32[1,4,32]{2,1,0:T(4,128)S(1)}, u32[]{:S(2)}, u32[]{:S(2)}) collective-permute-start(f32[1,4,32]{2,1,0:T(4,128)S(1)} %get-tuple-element.25), channel_id=1, source_target_pairs={{0,4},{4,8},{8,12},{12,16},{16,20},{20,24},{24,28},{1,5},{5,9},{9,... | collective-permute-start | bytes 1544 | tf_op jit(solution)/shard_map/ppermute | solution.py:19
  126.9 5.5 %collective-permute-start.5 = (f32[1,4,32]{2,1,0:T(4,128)S(1)}, f32[1,4,32]{2,1,0:T(4,128)S(1)}, u32[]{:S(2)}, u32[]{:S(2)}) collective-permute-start(f32[1,4,32]{2,1,0:T(4,128)S(1)} %get-tuple-element.26), channel_id=1, source_target_pairs={{4,0},{8,4},{12,8},{16,12},{20,16},{24,20},{28,24},{5,1},{9,5},{13... | collective-permute-start | bytes 1544 | tf_op jit(solution)/shard_map/ppermute | solution.py:22
  132.4 3.5 %collective-permute-start.6 = (f32[10,1,32]{2,1,0:T(1,128)S(1)}, f32[10,1,32]{2,1,0:T(1,128)S(1)}, u32[]{:S(2)}, u32[]{:S(2)}) collective-permute-start(f32[10,1,32]{2,1,0:T(1,128)S(1)} %get-tuple-element.19), channel_id=1, source_target_pairs={{0,1},{1,2},{2,3},{4,5},{5,6},{6,7},{8,9},{9,10},{10,11},{12,13},{... | collective-permute-start | bytes 3848 | tf_op jit(solution)/shard_map/ppermute | solution.py:19
  133.7 3.7 %collective-permute-start.7 = (f32[10,1,32]{2,1,0:T(1,128)S(1)}, f32[10,1,32]{2,1,0:T(1,128)S(1)}, u32[]{:S(2)}, u32[]{:S(2)}) collective-permute-start(f32[10,1,32]{2,1,0:T(1,128)S(1)} %get-tuple-element.20), channel_id=1, source_target_pairs={{1,0},{2,1},{3,2},{5,4},{6,5},{7,6},{9,8},{10,9},{11,10},{13,12},{... | collective-permute-start | bytes 3848 | tf_op jit(solution)/shard_map/ppermute | solution.py:22
  187.5 5.8 %collective-permute-start.8 = (f32[1,4,32]{2,1,0:T(4,128)S(1)}, f32[1,4,32]{2,1,0:T(4,128)S(1)}, u32[]{:S(2)}, u32[]{:S(2)}) collective-permute-start(f32[1,4,32]{2,1,0:T(4,128)S(1)} %get-tuple-element.23), channel_id=1, source_target_pairs={{0,4},{4,8},{8,12},{12,16},{16,20},{20,24},{24,28},{1,5},{5,9},{9,... | collective-permute-start | bytes 1544 | tf_op jit(solution)/shard_map/ppermute | solution.py:19
  192.0 5.5 %collective-permute-start.9 = (f32[1,4,32]{2,1,0:T(4,128)S(1)}, f32[1,4,32]{2,1,0:T(4,128)S(1)}, u32[]{:S(2)}, u32[]{:S(2)}) collective-permute-start(f32[1,4,32]{2,1,0:T(4,128)S(1)} %get-tuple-element.24), channel_id=1, source_target_pairs={{4,0},{8,4},{12,8},{16,12},{20,16},{24,20},{28,24},{5,1},{9,5},{13... | collective-permute-start | bytes 1544 | tf_op jit(solution)/shard_map/ppermute | solution.py:22
  197.5 3.5 %collective-permute-start.10 = (f32[10,1,32]{2,1,0:T(1,128)S(1)}, f32[10,1,32]{2,1,0:T(1,128)S(1)}, u32[]{:S(2)}, u32[]{:S(2)}) collective-permute-start(f32[10,1,32]{2,1,0:T(1,128)S(1)} %get-tuple-element.17), channel_id=1, source_target_pairs={{0,1},{1,2},{2,3},{4,5},{5,6},{6,7},{8,9},{9,10},{10,11},{12,13},{... | collective-permute-start | bytes 3848 | tf_op jit(solution)/shard_map/ppermute | solution.py:19
  198.8 3.8 %collective-permute-start.11 = (f32[10,1,32]{2,1,0:T(1,128)S(1)}, f32[10,1,32]{2,1,0:T(1,128)S(1)}, u32[]{:S(2)}, u32[]{:S(2)}) collective-permute-start(f32[10,1,32]{2,1,0:T(1,128)S(1)} %get-tuple-element.18), channel_id=1, source_target_pairs={{1,0},{2,1},{3,2},{5,4},{6,5},{7,6},{9,8},{10,9},{11,10},{13,12},{... | collective-permute-start | bytes 3848 | tf_op jit(solution)/shard_map/ppermute | solution.py:22
where the time goes:
time: 252 us; the launch traced here: 251 us
  blocking collectives  124 us (49%)
  starting transfers between devices  36.7 us (15%)
  waiting for transfers between devices  32.3 us (13%)
  matrix products  28.5 us (11%)
  local copies, waits for them, and re-layouts  12.6 us (5%)
  between operations  11.1 us (4%)
  other arithmetic  5.47 us (2%)
    psum x3, blocking collectives, two_products(): lax.psum((jnp.sum(values * values), jnp.sum(values * image)), ('gx', 'gy'))  124 us
    ppermute x6, waiting for transfers between devices, extended(): lax.ppermute(lax.slice_in_dim(block, 0, width, axis=dim), axis, backward)  17 us
    ppermute x6, starting transfers between devices, extended(): lax.ppermute(lax.slice_in_dim(block, block.shape[dim] - width, None, axis...  15.8 us
    all_to_all x1, waiting for transfers between devices, shards(): lax.all_to_all(sending, ('gx', 'gy'), split_axis=1, concat_axis=1, tiled=...  15.3 us
    ppermute x6, starting transfers between devices, extended(): lax.ppermute(lax.slice_in_dim(block, 0, width, axis=dim), axis, backward)  7.75 us
    all_to_all x1, starting transfers between devices, shards(): lax.all_to_all(target_rows, ('gx', 'gy'), split_axis=1, concat_axis=1, ti...  7.33 us
    dot_general x1, matrix products, shards(): jnp.einsum('ibd,bcd->ibc', blocks, choose, preferred_element_type=jnp.flo...  7.12 us
    dot_general x1, matrix products, shards(): jnp.einsum('bd,bcd->bc', target_blocks, choose, preferred_element_type=jn...  5.85 us
  transfers between devices with their start and end apart: 14, of which 7 were waited for; matrix products, arithmetic and copies ran while one was open for 6% of the time, Pallas kernels for 0%

commit v1 on v0

v1 whole, which is shorter than its diff:
```python
import functools

import jax
import jax.numpy as jnp
from jax import lax
from jax.experimental import pallas as pl
from jax.experimental.pallas import tpu as pltpu
from jax.sharding import PartitionSpec as P

BX = 8
BY = 4
ITERS = 3
LANES = 128
CHUNK = 8
MESH = pl.DeviceIdType.MESH

coupling_weight = 1.0


def kernel(
    gx,
    gy,
    feats_hbm,
    extra_hbm,
    adjacency_ref,
    voxel_hbm,
    reg_ref,
    solution_ref,
    residual_ref,
    got,
    got_extra,
    voxel,
    acc,
    vec,
    image,
    direction,
    carried,
    z_ref,
    my_ref,
    mid_ref,
    ym_ref,
    yp_ref,
    y_send,
    halo,
    part,
    parts,
    voxel_sem,
    feat_send,
    feat_recv,
    extra_send,
    extra_recv,
    halo_send,
    halo_recv,
    part_send,
    part_recv,
):
    count = gx * gy
    ix, iy = lax.axis_index("gx"), lax.axis_index("gy")
    me = ix * gy + iy
    feat, cols = got.shape[1], got.shape[2]
    bricks = vec.shape[0]
    slots = cols // bricks
    halves = cols // LANES
    per_half = LANES // slots

    def place(index):
        return (index // gy, index % gy)

    barrier = pltpu.get_barrier_semaphore()

    def greet(j, _):
        pl.semaphore_signal(
            barrier, inc=1, device_id=place((me + j) % count), device_id_type=MESH
        )
        return 0

    lax.fori_loop(1, count, greet, 0)
    voxel_copy = pltpu.make_async_copy(voxel_hbm, voxel, voxel_sem)
    voxel_copy.start()
    halo[...] = jnp.zeros_like(halo)
    acc[...] = jnp.zeros_like(acc)
    own_feat = pltpu.make_async_copy(
        feats_hbm.at[:, pl.ds(pl.multiple_of(me * cols, cols), cols)], got.at[me], feat_recv.at[me]
    )
    own_extra = pltpu.make_async_copy(extra_hbm.at[me], got_extra.at[me], extra_recv.at[me])
    own_feat.start()
    own_extra.start()
    pl.semaphore_wait(barrier, count - 1)

    def feat_copy(to, frm):
        return pltpu.make_async_remote_copy(
            src_ref=feats_hbm.at[:, pl.ds(pl.multiple_of(to * cols, cols), cols)],
            dst_ref=got.at[frm],
            send_sem=feat_send.at[to],
            recv_sem=feat_recv.at[frm],
            device_id=place(to),
            device_id_type=MESH,
        )

    def extra_copy(to, frm):
        return pltpu.make_async_remote_copy(
            src_ref=extra_hbm.at[to],
            dst_ref=got_extra.at[frm],
            send_sem=extra_send.at[to],
            recv_sem=extra_recv.at[frm],
            device_id=place(to),
            device_id_type=MESH,
        )

    def send(j, _):
        to = (me + j) % count
        feat_copy(to, me).start()
        extra_copy(to, me).start()
        return 0

    lax.fori_loop(1, count, send, 0)
    own_feat.wait()
    own_extra.wait()

    group = 4
    while count % group:
        group //= 2
    lane = lax.broadcasted_iota(jnp.int32, (1, group * LANES), 1)
    owner = (lane // slots) % per_half

    def absorb(g, _):
        sources = []
        for u in range(group):
            j = g * group + u
            source = (me + count - j) % count
            sources.append(source)
            if u:
                feat_copy(source, source).wait_recv()
                extra_copy(source, source).wait_recv()
            else:

                @pl.when(g > 0)
                def _():
                    feat_copy(source, source).wait_recv()
                    extra_copy(source, source).wait_recv()

        for h in range(halves):
            span = slice(h * LANES, (h + 1) * LANES)
            x = jnp.concatenate([got[s, :, span] for s in sources], axis=1)
            extra = jnp.concatenate(
                [got_extra[s, :, span].astype(jnp.float32) for s in sources], axis=1
            )
            live = extra[0:1]
            target = extra[1:2].astype(jnp.bfloat16)
            left = jnp.concatenate(
                [x * jnp.where(owner == b, live, 0.0).astype(jnp.bfloat16) for b in range(per_half)],
                axis=0,
            )
            right = jnp.concatenate(
                [
                    x,
                    jnp.broadcast_to(target, (16, group * LANES)),
                    jnp.zeros((LANES - feat - 16, group * LANES), jnp.bfloat16),
                ],
                axis=0,
            )
            rows = slice(h * per_half * feat, (h + 1) * per_half * feat)
            acc[rows, :] += lax.dot_general(
                left, right, (((1,), (1,)), ((), ())), preferred_element_type=jnp.float32
            )
        return 0

    lax.fori_loop(0, count // group, absorb, 0)
    voxel_copy.wait()

    eye = lax.broadcasted_iota(jnp.int32, (1, feat, LANES), 1) == lax.broadcasted_iota(
        jnp.int32, (1, feat, LANES), 2
    )
    chunks = bricks // CHUNK

    def at(t):
        return pl.ds(pl.multiple_of(t * CHUNK, CHUNK), CHUNK)

    def moment_at(t):
        rows = pl.ds(pl.multiple_of(t * CHUNK * feat, CHUNK * feat), CHUNK * feat)
        return acc[rows, :].reshape(CHUNK, feat, LANES)

    def begin(t, _):
        gathered = moment_at(t)[:, :, feat : feat + 1]
        vec[at(t), :] = jnp.sum(voxel[at(t)] * gathered, axis=1)
        return 0

    lax.fori_loop(0, chunks, begin, 0)

    masks = [adjacency_ref[:, k : k + 1] >= 0 for k in range(4)]
    degree = sum(jnp.where(m, 1.0, 0.0) for m in masks)
    here = [ix > 0, ix < gx - 1, iy > 0, iy < gy - 1]
    beside = [(ix - 1, iy), (ix + 1, iy), (ix, iy - 1), (ix, iy + 1)]

    def halo_copy(step, k):
        if k < 2:
            source = z_ref.at[step, pl.ds(k * (bricks - 8), 8)]
        else:
            source = y_send.at[step, k - 2]
        return pltpu.make_async_remote_copy(
            src_ref=source,
            dst_ref=halo.at[step, k ^ 1],
            send_sem=halo_send.at[step, k],
            recv_sem=halo_recv.at[step, k ^ 1],
            device_id=beside[k],
            device_id_type=MESH,
        )

    def halo_arrived(step, k):
        return pltpu.make_async_remote_copy(
            src_ref=y_send.at[step, 0],
            dst_ref=halo.at[step, k],
            send_sem=halo_send.at[step, k],
            recv_sem=halo_recv.at[step, k],
            device_id=beside[k],
            device_id_type=MESH,
        )

    def part_copy(step, to, frm):
        return pltpu.make_async_remote_copy(
            src_ref=part.at[step],
            dst_ref=parts.at[step, frm],
            send_sem=part_send.at[step, to],
            recv_sem=part_recv.at[step, frm],
            device_id=place(to),
            device_id_type=MESH,
        )

    def operate(step):
        def project(t, _):
            column = jnp.sum(voxel[at(t)] * vec[at(t), :][:, None, :], axis=2, keepdims=True)
            z_ref[step, at(t), :] = jnp.sum(jnp.where(eye, column, 0.0), axis=1)
            my_ref[at(t), :] = jnp.sum(moment_at(t) * column, axis=1)
            return 0

        lax.fori_loop(0, chunks, project, 0)
        for e in range(2):
            y_send[step, e] = z_ref[step, pl.ds(e * (BY - 1), BX, stride=BY), :]
        for k in range(4):

            @pl.when(here[k])
            def _():
                halo_copy(step, k).start()

        z = z_ref[step]
        ym_ref[1:bricks, :] = z[: bricks - 1]
        yp_ref[0 : bricks - 1, :] = z[1:]
        for k in range(4):

            @pl.when(here[k])
            def _():
                halo_arrived(step, k).wait_recv()

        xm = jnp.concatenate([halo[step, 0][8 - BY :], z[: bricks - BY]], axis=0)
        xp = jnp.concatenate([z[BY:], halo[step, 1][:BY]], axis=0)
        ym_ref[pl.ds(0, BX, stride=BY), :] = halo[step, 2]
        yp_ref[pl.ds(BY - 1, BX, stride=BY), :] = halo[step, 3]
        near = jnp.where(masks[0], xm, 0.0) + jnp.where(masks[1], xp, 0.0)
        near = near + jnp.where(masks[2], ym_ref[...], 0.0) + jnp.where(masks[3], yp_ref[...], 0.0)
        mid_ref[...] = my_ref[...] + coupling_weight * (degree * z - near)

        def expand(t, _):
            column = jnp.sum(
                jnp.where(eye, mid_ref[at(t), :][:, None, :], 0.0), axis=2, keepdims=True
            )
            back = jnp.sum(voxel[at(t)] * column, axis=1)
            image[at(t), :] = back + reg_ref[at(t), :] * vec[at(t), :]
            return 0

        lax.fori_loop(0, chunks, expand, 0)

    def fold(values):
        total = jnp.sum(values, axis=0, keepdims=True)
        width = total.shape[1]
        return sum(total[:, c : c + LANES] for c in range(0, width, LANES))

    def two_products(step):
        r, w = vec[...], image[...]
        mine = jnp.concatenate([fold(r * r), fold(r * w)], axis=0)
        part[step] = mine
        parts[step, me] = mine

        def start(j, _):
            part_copy(step, (me + j) % count, me).start()
            return 0

        lax.fori_loop(1, count, start, 0)

        def finish(j, _):
            source = (me + count - j) % count
            part_copy(step, source, source).wait_recv()
            return 0

        lax.fori_loop(1, count, finish, 0)
        total = jnp.sum(jnp.sum(parts[step], axis=0), axis=1, keepdims=True)
        return total[0:1], total[1:2]

    norm_now = alpha = None
    for step in range(ITERS):
        operate(step)
        norm, product = two_products(step)
        if step == 0:
            alpha = norm / product
            d, c = vec[...], image[...]
            solution_ref[...] = alpha * d
        else:
            ratio = norm / norm_now
            alpha = norm / (product - ratio * norm / alpha)
            d = vec[...] + ratio * direction[...]
            c = image[...] + ratio * carried[...]
            solution_ref[...] += alpha * d
        r = vec[...] - alpha * c
        if step + 1 < ITERS:
            vec[...] = r
            direction[...] = d
            carried[...] = c
        else:
            residual_ref[...] = r
        norm_now = norm

    def drain(j, _):
        to = (me + j) % count
        feat_copy(to, me).wait_send()
        extra_copy(to, me).wait_send()
        for step in range(ITERS):
            part_copy(step, to, me).wait_send()
        return 0

    lax.fori_loop(1, count, drain, 0)
    for step in range(ITERS):
        for k in range(4):

            @pl.when(here[k])
            def _():
                halo_copy(step, k).wait_send()


def shards(gx, gy, point_feats, point_targets, point_lists, brick_adjacency, voxel_feats, voxel_reg):
    feat = point_feats.shape[0]
    brick_total, slots = point_lists.shape
    bricks, _, vox = voxel_feats.shape
    count = gx * gy
    cols = bricks * slots
    offset = point_lists - jnp.arange(brick_total, dtype=jnp.int32)[:, None] * slots
    offset = jnp.where(point_lists >= 0, offset, -1)
    live = jnp.any(
        offset[:, :, None] == jnp.arange(slots, dtype=jnp.int32)[None, None, :], axis=1
    ).astype(jnp.bfloat16)
    extra = jnp.stack([live.reshape(count, cols), point_targets.reshape(count, cols)], axis=1)
    vmem = pl.BlockSpec(memory_space=pltpu.VMEM)
    hbm = pl.BlockSpec(memory_space=pl.ANY)
    f32 = jnp.float32
    return pl.pallas_call(
        functools.partial(kernel, gx, gy),
        out_shape=(jax.ShapeDtypeStruct((bricks, vox), f32),) * 2,
        in_specs=[hbm, hbm, vmem, hbm, vmem],
        out_specs=(vmem, vmem),
        scratch_shapes=[
            pltpu.VMEM((count, feat, cols), jnp.bfloat16),
            pltpu.VMEM((count, 2, cols), jnp.bfloat16),
            pltpu.VMEM((bricks, feat, vox), f32),
            pltpu.VMEM((bricks * feat, LANES), f32),
            pltpu.VMEM((bricks, vox), f32),
            pltpu.VMEM((bricks, vox), f32),
            pltpu.VMEM((bricks, vox), f32),
            pltpu.VMEM((bricks, vox), f32),
            pltpu.VMEM((ITERS, bricks, LANES), f32),
            pltpu.VMEM((bricks, LANES), f32),
            pltpu.VMEM((bricks, LANES), f32),
            pltpu.VMEM((bricks, LANES), f32),
            pltpu.VMEM((bricks, LANES), f32),
            pltpu.VMEM((ITERS, 2, BX, LANES), f32),
            pltpu.VMEM((ITERS, 4, 8, LANES), f32),
            pltpu.VMEM((ITERS, 2, LANES), f32),
            pltpu.VMEM((ITERS, count, 2, LANES), f32),
            pltpu.SemaphoreType.DMA,
            pltpu.SemaphoreType.DMA((count,)),
            pltpu.SemaphoreType.DMA((count,)),
            pltpu.SemaphoreType.DMA((count,)),
            pltpu.SemaphoreType.DMA((count,)),
            pltpu.SemaphoreType.DMA((ITERS, 4)),
            pltpu.SemaphoreType.DMA((ITERS, 4)),
            pltpu.SemaphoreType.DMA((ITERS, count)),
            pltpu.SemaphoreType.DMA((ITERS, count)),
        ],
        compiler_params=pltpu.CompilerParams(collective_id=0, has_side_effects=True),
    )(point_feats, extra, brick_adjacency, voxel_feats, voxel_reg)


def solution(mesh):
    placed = (
        P(None, ("gx", "gy")),
        P(("gx", "gy")),
        P(("gx", "gy"), None),
        P(("gx", "gy"), None),
        P(("gx", "gy"), None, None),
        P(("gx", "gy"), None),
    )
    return jax.shard_map(
        functools.partial(shards, mesh.shape["gx"], mesh.shape["gy"]),
        mesh=mesh,
        in_specs=placed,
        out_specs=(P(("gx", "gy"), None), P(("gx", "gy"), None)),
        check_vma=False,
    )
```

time: 252 us -> 62.7 us (0.25)
  blocking collectives: 124 us -> 0 us
  Pallas kernels: 0 us -> 54.7 us
  starting transfers between devices: 36.7 us -> 0 us
  waiting for transfers between devices: 32.3 us -> 0 us
  matrix products: 28.5 us -> 0 us
  between operations: 11.1 us -> 0.67 us
  local copies, waits for them, and re-layouts: 12.6 us -> 5.47 us
  other arithmetic: 5.47 us -> 1.51 us
    psum x3 -> x0, blocking collectives: 124 us -> none  [two_products(): lax.psum((jnp.sum(values * values), jnp.sum(values * image)), ('gx', 'gy'))]
    pallas_call x0 -> x1, Pallas kernels: none -> 54.7 us  [shards(): pl.pallas_call(functools.partial(kernel, gx, gy), out_shape=(jax.ShapeDty...]
    dot_general x14 -> x0, matrix products: 28.5 us -> none  [the longest x1 7.12 us: shards(): jnp.einsum('ibd,bcd->ibc', blocks, choose, preferred_element_type=jnp.flo...]
    ppermute x12 -> x0, starting transfers between devices: 23.5 us -> none  [the longest x6 15.8 us: extended(): lax.ppermute(lax.slice_in_dim(block, block.shape[dim] - width, None, axis...]
    ppermute x12 -> x0, waiting for transfers between devices: 17 us -> none  [the longest x6 17 us: extended(): lax.ppermute(lax.slice_in_dim(block, 0, width, axis=dim), axis, backward)]
    all_to_all x2 -> x0, waiting for transfers between devices: 15.3 us -> none  [the longest x1 15.3 us: shards(): lax.all_to_all(sending, ('gx', 'gy'), split_axis=1, concat_axis=1, tiled=...]
    all_to_all x2 -> x0, starting transfers between devices: 13.2 us -> none  [the longest x1 7.33 us: shards(): lax.all_to_all(target_rows, ('gx', 'gy'), split_axis=1, concat_axis=1, ti...]
    reshape x4 -> x0, local copies, waits for them, and re-layouts: 5 us -> none  [the longest x1 2.58 us: shards(): sending = picked.reshape(feat_count, devices, local_bricks * slots)]
  transfers between devices with their start and end apart: 14 -> 0, of which waited for: 7 -> 0; matrix products, arithmetic and copies ran while one was open for 6% -> 0% of each run, Pallas kernels for 0% -> 0%
where the time goes in v1:
time: 62.7 us; the launch traced here: 62.3 us
  Pallas kernels  54.7 us (87%)
  local copies, waits for them, and re-layouts  5.47 us (9%)
  other arithmetic  1.51 us (2%)
  between operations  0.67 us (1%)
    pallas_call x1, Pallas kernels, shards(): pl.pallas_call(functools.partial(kernel, gx, gy), out_shape=(jax.ShapeDty...  54.7 us
    unnamed x3, local copies, waits for them, and re-layouts  4.31 us

profile of v1, /device:TPU:0, one launch (start us, length us, event | category | flops | bytes accessed | tf_op | source)
XLA Modules:
  0.0 62.3 jit_solution(7465162647077066238)
XLA Ops:
  0.6 0.8 %subtract_select_fusion = s32[1024,8]{0,1:T(8,128)S(1)} fusion(s32[1024,8]{0,1:T(8,128)} %param.8, s32[1024]{0:T(1024)S(1)} %iota_multiply_fusion), kind=kLoop, calls=%fused_computation.3 | loop fusion | flops 24576 | bytes 69632 | tf_op jit(solution)/shard_map/jit(_where)/select_n | solution.py:345
  1.5 0.2 copy.14
  1.6 0.3 reshape.23
  1.9 0.7 %stack_reshape.5 = bf16[32,1,256]{2,1,0:T(2,128)(2,1)S(1)} reshape(bf16[8192]{0:T(1024)(128)(2,1)} %param.7) | data formatting | bytes 32768 | tf_op jit(solution)/shard_map/stack;reshape | solution.py:349
  2.6 0.7 %pad_maximum_fusion.extra_hbm = bf16[32,2,256]{2,1,0:T(2,128)(2,1)} fusion(bf16[32,1,256]{2,1,0:T(2,128)(2,1)S(1)} %stack_reshape.5, bf16[32,1,256]{2,1,0:T(2,128)(2,1)S(1)} %reshape.23), kind=kLoop, calls=%fused_computation.2 | loop fusion | flops 65536 | bytes 65536 | tf_op jit(solution)/shard_map/stack | solution.py:349
  3.3 1.4 %copy.17.adjacency_ref = s32[32,4]{1,0:T(8,128)} copy(s32[32,4]{0,1:T(4,128)} %param.9) | data formatting | bytes 1024 | tf_op args[3]
  4.7 54.7 %shard_map.77 = (f32[32,512]{1,0:T(8,128)}, f32[32,512]{1,0:T(8,128)}) custom-call(bf16[32,8192]{1,0:T(8,128)(2,1)} %feats_hbm.1, bf16[32,2,256]{2,1,0:T(2,128)(2,1)} %pad_maximum_fusion.extra_hbm, s32[32,4]{1,0:T(8,128)} %copy.17.adjacency_ref, f32[32,32,512]{2,1,0:T(8,128)} %voxel_hbm.1, f32[32,512]{1,0:T(8,128)} %reg_ref.1), custom_call_target="tpu_custom_call" | custom-call | tf_op jit(solution)/shard_map/pallas_call | solution.py:353
  59.3 1.5 %copy.20 = f32[32,512]{1,0:T(8,128)} copy(f32[32,512]{1,0:T(8,128)} %get-tuple-element.4) | data formatting | bytes 131072
  60.8 1.5 %copy.21 = f32[32,512]{1,0:T(8,128)} copy(f32[32,512]{1,0:T(8,128)} %get-tuple-element.5) | data formatting | bytes 131072
  (3 shorter events, 0.0 us)

commit v2 on v1

--- a/solution.py
+++ b/solution.py
@@ -1,4 +1,5 @@
 import functools
+import math
 
 import jax
 import jax.numpy as jnp
@@ -13,6 +14,9 @@
 LANES = 128
 CHUNK = 8
 MESH = pl.DeviceIdType.MESH
+STRIDE = 1
+SCALE = 2.0**-8
+SHIFTS = (8.0, 1.0, 4.0)
 
 coupling_weight = 1.0
 
@@ -21,7 +25,8 @@
     gx,
     gy,
     feats_hbm,
-    extra_hbm,
+    target_ref,
+    lists_ref,
     adjacency_ref,
     voxel_hbm,
     reg_ref,
@@ -29,12 +34,11 @@
     residual_ref,
     got,
     got_extra,
+    extra,
+    flat,
     voxel,
     acc,
-    vec,
-    image,
-    direction,
-    carried,
+    basis,
     z_ref,
     my_ref,
     mid_ref,
@@ -58,11 +62,13 @@
     ix, iy = lax.axis_index("gx"), lax.axis_index("gy")
     me = ix * gy + iy
     feat, cols = got.shape[1], got.shape[2]
-    bricks = vec.shape[0]
+    bricks = reg_ref.shape[0]
     slots = cols // bricks
     halves = cols // LANES
     per_half = LANES // slots
 
+    step_by = STRIDE if math.gcd(STRIDE, count) == 1 else 1
+
     def place(index):
         return (index // gy, index % gy)
 
@@ -70,7 +76,7 @@
 
     def greet(j, _):
         pl.semaphore_signal(
-            barrier, inc=1, device_id=place((me + j) % count), device_id_type=MESH
+            barrier, inc=1, device_id=place((me + j * step_by) % count), device_id_type=MESH
         )
         return 0
 
@@ -82,8 +88,45 @@
     own_feat = pltpu.make_async_copy(
         feats_hbm.at[:, pl.ds(pl.multiple_of(me * cols, cols), cols)], got.at[me], feat_recv.at[me]
     )
-    own_extra = pltpu.make_async_copy(extra_hbm.at[me], got_extra.at[me], extra_recv.at[me])
+    own_extra = pltpu.make_async_copy(extra.at[me], got_extra.at[me], extra_recv.at[me])
     own_feat.start()
+
+    total_bricks = lists_ref.shape[1]
+    groups = total_bricks // LANES
+    wide = slots * LANES
+    listed = lists_ref[...]
+    offset = listed - slots * lax.broadcasted_iota(jnp.int32, listed.shape, 1)
+    offset = jnp.where(listed >= 0, offset, -1)
+    hits = jnp.concatenate(
+        [
+            jnp.max(jnp.where(offset == d, 1.0, 0.0), axis=0, keepdims=True)
+            for d in range(slots)
+        ],
+        axis=0,
+    )
+    hits = jnp.concatenate(
+        [hits[:, g * LANES : (g + 1) * LANES] for g in range(groups)], axis=0
+    ).astype(jnp.bfloat16)
+    spread = jnp.where(
+        lax.broadcasted_iota(jnp.int32, (LANES, wide), 1) // slots
+        == lax.broadcasted_iota(jnp.int32, (LANES, wide), 0),
+        1.0,
+        0.0,
+    ).astype(jnp.bfloat16)
+    spread_hits = jnp.dot(hits, spread, preferred_element_type=jnp.float32)
+    same = (
+        lax.broadcasted_iota(jnp.int32, (slots, wide), 1) % slots
+        == lax.broadcasted_iota(jnp.int32, (slots, wide), 0)
+    )
+    live_rows = jnp.sum(
+        jnp.where(same[None], spread_hits.reshape(groups, slots, wide), 0.0), axis=1
+    )
+    for l in range(slots):
+        flat[pl.ds(l, groups, stride=slots), :] = live_rows[:, l * LANES : (l + 1) * LANES]
+    targets = target_ref[...].astype(jnp.float32)
+    for k in range(count):
+        rows = slice(k * halves, (k + 1) * halves)
+        extra[k] = jnp.concatenate([flat[rows, :], targets[rows]], axis=0).astype(jnp.bfloat16)
     own_extra.start()
     pl.semaphore_wait(barrier, count - 1)
 
@@ -99,7 +142,7 @@
 
     def extra_copy(to, frm):
         return pltpu.make_async_remote_copy(
-            src_ref=extra_hbm.at[to],
+            src_ref=extra.at[to],
             dst_ref=got_extra.at[frm],
             send_sem=extra_send.at[to],
             recv_sem=extra_recv.at[frm],
@@ -108,7 +151,7 @@
         )
 
     def send(j, _):
-        to = (me + j) % count
+        to = (me + j * step_by) % count
         feat_copy(to, me).start()
         extra_copy(to, me).start()
         return 0
@@ -127,7 +170,7 @@
         sources = []
         for u in range(group):
             j = g * group + u
-            source = (me + count - j) % count
+            source = (me + (count - j) * step_by) % count
             sources.append(source)
             if u:
                 feat_copy(source, source).wait_recv()
@@ -142,11 +185,11 @@
         for h in range(halves):
             span = slice(h * LANES, (h + 1) * LANES)
             x = jnp.concatenate([got[s, :, span] for s in sources], axis=1)
-            extra = jnp.concatenate(
-                [got_extra[s, :, span].astype(jnp.float32) for s in sources], axis=1
+            more = jnp.concatenate(
+                [got_extra[s].astype(jnp.float32) for s in sources], axis=1
             )
-            live = extra[0:1]
-            target = extra[1:2].astype(jnp.bfloat16)
+            live = more[h : h + 1]
+            target = more[halves + h : halves + h + 1].astype(jnp.bfloat16)
             left = jnp.concatenate(
                 [x * jnp.where(owner == b, live, 0.0).astype(jnp.bfloat16) for b in range(per_half)],
                 axis=0,
@@ -182,13 +225,21 @@
 
     def begin(t, _):
         gathered = moment_at(t)[:, :, feat : feat + 1]
-        vec[at(t), :] = jnp.sum(voxel[at(t)] * gathered, axis=1)
+        basis[0, at(t), :] = jnp.sum(voxel[at(t)] * gathered, axis=1)
         return 0
 
     lax.fori_loop(0, chunks, begin, 0)
 
-    masks = [adjacency_ref[:, k : k + 1] >= 0 for k in range(4)]
-    degree = sum(jnp.where(m, 1.0, 0.0) for m in masks)
+    linked = jnp.where(adjacency_ref[...] >= 0, 1.0, 0.0)
+    same_brick = lax.broadcasted_iota(jnp.int32, (bricks, bricks), 0) == lax.broadcasted_iota(
+        jnp.int32, (bricks, bricks), 1
+    )
+    weights = [
+        jnp.sum(jnp.where(same_brick, linked[k : k + 1], 0.0), axis=1, keepdims=True)
+        for k in range(4)
+    ]
+    masks = [w > 0.0 for w in weights]
+    degree = weights[0] + weights[1] + weights[2] + weights[3]
     here = [ix > 0, ix < gx - 1, iy > 0, iy < gy - 1]
     beside = [(ix - 1, iy), (ix + 1, iy), (ix, iy - 1), (ix, iy + 1)]
 
@@ -216,19 +267,19 @@
             device_id_type=MESH,
         )
 
-    def part_copy(step, to, frm):
+    def part_copy(to, frm):
         return pltpu.make_async_remote_copy(
-            src_ref=part.at[step],
-            dst_ref=parts.at[step, frm],
-            send_sem=part_send.at[step, to],
-            recv_sem=part_recv.at[step, frm],
+            src_ref=part,
+            dst_ref=parts.at[frm],
+            send_sem=part_send.at[to],
+            recv_sem=part_recv.at[frm],
             device_id=place(to),
             device_id_type=MESH,
         )
 
     def operate(step):
         def project(t, _):
-            column = jnp.sum(voxel[at(t)] * vec[at(t), :][:, None, :], axis=2, keepdims=True)
+            column = jnp.sum(voxel[at(t)] * basis[step, at(t), :][:, None, :], axis=2, keepdims=True)
             z_ref[step, at(t), :] = jnp.sum(jnp.where(eye, column, 0.0), axis=1)
             my_ref[at(t), :] = jnp.sum(moment_at(t) * column, axis=1)
             return 0
@@ -264,7 +315,8 @@
                 jnp.where(eye, mid_ref[at(t), :][:, None, :], 0.0), axis=2, keepdims=True
             )
             back = jnp.sum(voxel[at(t)] * column, axis=1)
-            image[at(t), :] = back + reg_ref[at(t), :] * vec[at(t), :]
+            shifted = (reg_ref[at(t), :] - SHIFTS[step]) * basis[step, at(t), :]
+            basis[step + 1, at(t), :] = SCALE * (back + shifted)
             return 0
 
         lax.fori_loop(0, chunks, expand, 0)
@@ -274,56 +326,81 @@
         width = total.shape[1]
         return sum(total[:, c : c + LANES] for c in range(0, width, LANES))
 
-    def two_products(step):
-        r, w = vec[...], image[...]
-        mine = jnp.concatenate([fold(r * r), fold(r * w)], axis=0)
-        part[step] = mine
-        parts[step, me] = mine
-
-        def start(j, _):
-            part_copy(step, (me + j) % count, me).start()
-            return 0
-
-        lax.fori_loop(1, count, start, 0)
-
-        def finish(j, _):
-            source = (me + count - j) % count
-            part_copy(step, source, source).wait_recv()
-            return 0
-
-        lax.fori_loop(1, count, finish, 0)
-        total = jnp.sum(jnp.sum(parts[step], axis=0), axis=1, keepdims=True)
-        return total[0:1], total[1:2]
-
-    norm_now = alpha = None
     for step in range(ITERS):
         operate(step)
-        norm, product = two_products(step)
-        if step == 0:
-            alpha = norm / product
-            d, c = vec[...], image[...]
-            solution_ref[...] = alpha * d
-        else:
-            ratio = norm / norm_now
-            alpha = norm / (product - ratio * norm / alpha)
-            d = vec[...] + ratio * direction[...]
-            c = image[...] + ratio * carried[...]
-            solution_ref[...] += alpha * d
-        r = vec[...] - alpha * c
+
+    pairs = [(a, b) for a in range(ITERS) for b in range(a, ITERS + 1)]
+    rows = [fold(basis[a] * basis[b]) for a, b in pairs]
+    rows = rows + [jnp.zeros_like(rows[0])] * (-len(rows) % 8)
+    sums = jnp.sum(jnp.concatenate(rows, axis=0), axis=1, keepdims=True)
+    entry = lax.broadcasted_iota(jnp.int32, (len(rows), LANES), 1)
+    diagonal = entry == lax.broadcasted_iota(jnp.int32, (len(rows), LANES), 0)
+    mine = jnp.sum(jnp.where(diagonal, sums, 0.0), axis=0, keepdims=True)
+    part[...] = mine
+    parts[me] = mine
+
+    def start(j, _):
+        part_copy((me + j * step_by) % count, me).start()
+        return 0
+
+    lax.fori_loop(1, count, start, 0)
+
+    def finish(j, _):
+        source = (me + (count - j) * step_by) % count
+        part_copy(source, source).wait_recv()
+        return 0
+
+    lax.fori_loop(1, count, finish, 0)
+    total = jnp.sum(parts[...], axis=0)
+    spread_total = jnp.sum(
+        jnp.where(diagonal, jnp.broadcast_to(total, diagonal.shape), 0.0), axis=1, keepdims=True
+    )
+    gram = {}
+    for e, (a, b) in enumerate(pairs):
+        gram[a, b] = gram[b, a] = spread_total[e : e + 1]
+
+    def inner(left, right):
+        terms = [
+            left[a] * right[b] * gram[a, b] for a in range(len(left)) for b in range(len(right))
+        ]
+        return functools.reduce(lambda p, q: p + q, terms)
+
+    def apply(coefficients):
+        size = len(coefficients)
+        out = [SHIFTS[k] * coefficients[k] for k in range(size)]
+        out.append(coefficients[-1] * (1.0 / SCALE))
+        for k in range(1, size):
+            out[k] = out[k] + coefficients[k - 1] * (1.0 / SCALE)
+        return out
+
+    one = jnp.ones((1, 1), jnp.float32)
+    res, direction, answer = [one], [one], []
+    norm_now = gram[0, 0]
+    for step in range(ITERS):
+        image = apply(direction)
+        alpha = norm_now / inner(direction, image)
+        padded = answer + [jnp.zeros_like(one)] * (len(direction) - len(answer))
+        answer = [p + alpha * d for p, d in zip(padded, direction)]
+        res = [p - alpha * w for p, w in zip(res + [jnp.zeros_like(one)], image)]
         if step + 1 < ITERS:
-            vec[...] = r
-            direction[...] = d
-            carried[...] = c
-        else:
-            residual_ref[...] = r
-        norm_now = norm
+            norm_next = inner(res, res)
+            ratio = norm_next / norm_now
+            direction = [
+                p + ratio * d for p, d in zip(res, direction + [jnp.zeros_like(one)])
+            ]
+            norm_now = norm_next
+    solution_ref[...] = functools.reduce(
+        lambda p, q: p + q, [c * basis[k] for k, c in enumerate(answer)]
+    )
+    residual_ref[...] = functools.reduce(
+        lambda p, q: p + q, [c * basis[k] for k, c in enumerate(res)]
+    )
 
     def drain(j, _):
-        to = (me + j) % count
+        to = (me + j * step_by) % count
         feat_copy(to, me).wait_send()
         extra_copy(to, me).wait_send()
-        for step in range(ITERS):
-            part_copy(step, to, me).wait_send()
+        part_copy(to, me).wait_send()
         return 0
 
     lax.fori_loop(1, count, drain, 0)
@@ -341,29 +418,22 @@
     bricks, _, vox = voxel_feats.shape
     count = gx * gy
     cols = bricks * slots
-    offset = point_lists - jnp.arange(brick_total, dtype=jnp.int32)[:, None] * slots
-    offset = jnp.where(point_lists >= 0, offset, -1)
-    live = jnp.any(
-        offset[:, :, None] == jnp.arange(slots, dtype=jnp.int32)[None, None, :], axis=1
-    ).astype(jnp.bfloat16)
-    extra = jnp.stack([live.reshape(count, cols), point_targets.reshape(count, cols)], axis=1)
     vmem = pl.BlockSpec(memory_space=pltpu.VMEM)
     hbm = pl.BlockSpec(memory_space=pl.ANY)
     f32 = jnp.float32
     return pl.pallas_call(
         functools.partial(kernel, gx, gy),
         out_shape=(jax.ShapeDtypeStruct((bricks, vox), f32),) * 2,
-        in_specs=[hbm, hbm, vmem, hbm, vmem],
+        in_specs=[hbm, vmem, vmem, vmem, hbm, vmem],
         out_specs=(vmem, vmem),
         scratch_shapes=[
             pltpu.VMEM((count, feat, cols), jnp.bfloat16),
-            pltpu.VMEM((count, 2, cols), jnp.bfloat16),
+            pltpu.VMEM((count, 2 * cols // LANES, LANES), jnp.bfloat16),
+            pltpu.VMEM((count, 2 * cols // LANES, LANES), jnp.bfloat16),
+            pltpu.VMEM((count * cols // LANES, LANES), f32),
             pltpu.VMEM((bricks, feat, vox), f32),
             pltpu.VMEM((bricks * feat, LANES), f32),
-            pltpu.VMEM((bricks, vox), f32),
-            pltpu.VMEM((bricks, vox), f32),
-            pltpu.VMEM((bricks, vox), f32),
-            pltpu.VMEM((bricks, vox), f32),
+            pltpu.VMEM((ITERS + 1, bricks, vox), f32),
             pltpu.VMEM((ITERS, bricks, LANES), f32),
             pltpu.VMEM((bricks, LANES), f32),
             pltpu.VMEM((bricks, LANES), f32),
@@ -371,8 +441,8 @@
             pltpu.VMEM((bricks, LANES), f32),
             pltpu.VMEM((ITERS, 2, BX, LANES), f32),
             pltpu.VMEM((ITERS, 4, 8, LANES), f32),
-            pltpu.VMEM((ITERS, 2, LANES), f32),
-            pltpu.VMEM((ITERS, count, 2, LANES), f32),
+            pltpu.VMEM((1, LANES), f32),
+            pltpu.VMEM((count, 1, LANES), f32),
             pltpu.SemaphoreType.DMA,
             pltpu.SemaphoreType.DMA((count,)),
             pltpu.SemaphoreType.DMA((count,)),
@@ -380,11 +450,18 @@
             pltpu.SemaphoreType.DMA((count,)),
             pltpu.SemaphoreType.DMA((ITERS, 4)),
             pltpu.SemaphoreType.DMA((ITERS, 4)),
-            pltpu.SemaphoreType.DMA((ITERS, count)),
-            pltpu.SemaphoreType.DMA((ITERS, count)),
+            pltpu.SemaphoreType.DMA((count,)),
+            pltpu.SemaphoreType.DMA((count,)),
         ],
         compiler_params=pltpu.CompilerParams(collective_id=0, has_side_effects=True),
-    )(point_feats, extra, brick_adjacency, voxel_feats, voxel_reg)
+    )(
+        point_feats,
+        point_targets.reshape(-1, LANES),
+        point_lists.T,
+        brick_adjacency.T,
+        voxel_feats,
+        voxel_reg,
+    )
 
 
 def solution(mesh):

time: 62.7 us -> 48.2 us (0.77)
  Pallas kernels: 54.7 us -> 44.4 us
  local copies, waits for them, and re-layouts: 5.47 us -> 2.95 us
  other arithmetic: 1.51 us -> 0 us
    pallas_call x1, Pallas kernels: 54.7 us -> 44.4 us  [shards(): pl.pallas_call(functools.partial(kernel, gx, gy), out_shape=(jax.ShapeDty...]
    unnamed x3 -> x2, local copies, waits for them, and re-layouts: 4.31 us -> 2.95 us
    select_n x1 -> x0, other arithmetic: 0.77 us -> none  [shards(): offset = jnp.where(point_lists >= 0, offset, -1)]
    another operation x1 -> x0, local copies, waits for them, and re-layouts: 0.73 us -> none  [shards(): jnp.stack([live.reshape(count, cols), point_targets.reshape(count, cols)]...]
    another operation x1 -> x0, other arithmetic: 0.69 us -> none  [shards(): jnp.stack([live.reshape(count, cols), point_targets.reshape(count, cols)]...]
where the time goes in v2:
time: 48.2 us; the launch traced here: 47.9 us
  Pallas kernels  44.4 us (92%)
  local copies, waits for them, and re-layouts  2.95 us (6%)
  between operations  0.64 us (1%)
    pallas_call x1, Pallas kernels, shards(): pl.pallas_call(functools.partial(kernel, gx, gy), out_shape=(jax.ShapeDty...  44.4 us
    unnamed x2, local copies, waits for them, and re-layouts  2.95 us

profile of v2, /device:TPU:0, one launch (start us, length us, event | category | flops | bytes accessed | tf_op | source)
XLA Modules:
  0.0 47.9 jit_solution(6748557510224152258)
XLA Ops:
  0.6 44.4 %shard_map.77 = (f32[32,512]{1,0:T(8,128)}, f32[32,512]{1,0:T(8,128)}) custom-call(bf16[32,8192]{1,0:T(8,128)(2,1)} %feats_hbm.1, bf16[64,128]{1,0:T(8,128)(2,1)} %bitcast.4, s32[8,1024]{1,0:T(8,128)} %bitcast.3, s32[4,32]{1,0:T(4,128)} %bitcast.5, f32[32,32,512]{2,1,0:T(8,128)} %voxel_hbm.1, f32[32,512]{1,0:T(8,128)} %reg_ref.1), custom_call_target="tpu_custom_call" | custom-call | tf_op jit(solution)/shard_map/pallas_call | solution.py:424
  45.0 1.5 %copy.10 = f32[32,512]{1,0:T(8,128)} copy(f32[32,512]{1,0:T(8,128)} %get-tuple-element.4) | data formatting | bytes 131072
  46.5 1.5 %copy.11 = f32[32,512]{1,0:T(8,128)} copy(f32[32,512]{1,0:T(8,128)} %get-tuple-element.5) | data formatting | bytes 131072

commit v3 on v2

--- a/solution.py
+++ b/solution.py
@@ -14,7 +14,7 @@
 LANES = 128
 CHUNK = 8
 MESH = pl.DeviceIdType.MESH
-STRIDE = 1
+STRIDE = 11
 SCALE = 2.0**-8
 SHIFTS = (8.0, 1.0, 4.0)
 
@@ -30,16 +30,21 @@
     adjacency_ref,
     voxel_hbm,
     reg_ref,
-    solution_ref,
-    residual_ref,
+    answer_ref,
+    res_ref,
+    direction_ref,
+    image_ref,
+    alpha_ref,
     got,
     got_extra,
     extra,
     flat,
     voxel,
     acc,
+    square,
     basis,
     z_ref,
+    q_ref,
     my_ref,
     mid_ref,
     ym_ref,
@@ -157,6 +162,23 @@
         return 0
 
     lax.fori_loop(1, count, send, 0)
+    voxel_copy.wait()
+    square[...] = jnp.zeros_like(square)
+
+    def squares(t, _):
+        for u in range(4):
+            b = t * 4 + u
+            rows = pl.ds(pl.multiple_of(b * feat, feat), feat)
+            square[rows, 0:feat] = lax.dot_general(
+                voxel[b],
+                voxel[b],
+                (((1,), (1,)), ((), ())),
+                precision=lax.Precision.HIGHEST,
+                preferred_element_type=jnp.float32,
+            )
+        return 0
+
+    lax.fori_loop(0, bricks // 4, squares, 0)
     own_feat.wait()
     own_extra.wait()
 
@@ -209,7 +231,6 @@
         return 0
 
     lax.fori_loop(0, count // group, absorb, 0)
-    voxel_copy.wait()
 
     eye = lax.broadcasted_iota(jnp.int32, (1, feat, LANES), 1) == lax.broadcasted_iota(
         jnp.int32, (1, feat, LANES), 2
@@ -219,13 +240,18 @@
     def at(t):
         return pl.ds(pl.multiple_of(t * CHUNK, CHUNK), CHUNK)
 
-    def moment_at(t):
+    def block(ref, t):
         rows = pl.ds(pl.multiple_of(t * CHUNK * feat, CHUNK * feat), CHUNK * feat)
-        return acc[rows, :].reshape(CHUNK, feat, LANES)
+        return ref[rows, :].reshape(CHUNK, feat, LANES)
+
+    def as_column(rows):
+        return jnp.sum(jnp.where(eye, rows[:, None, :], 0.0), axis=2, keepdims=True)
+
+    def gathered(t):
+        return block(acc, t)[:, :, feat : feat + 1]
 
     def begin(t, _):
-        gathered = moment_at(t)[:, :, feat : feat + 1]
-        basis[0, at(t), :] = jnp.sum(voxel[at(t)] * gathered, axis=1)
+        z_ref[0, at(t), :] = jnp.sum(block(square, t) * gathered(t), axis=1)
         return 0
 
     lax.fori_loop(0, chunks, begin, 0)
@@ -277,14 +303,19 @@
             device_id_type=MESH,
         )
 
+    def fold(values):
+        total = jnp.sum(values, axis=0, keepdims=True)
+        width = total.shape[1]
+        return sum(total[:, c : c + LANES] for c in range(0, width, LANES))
+
+    def next_basis(step, t):
+        if step == 0:
+            return jnp.sum(voxel[at(t)] * gathered(t), axis=1)
+        back = jnp.sum(voxel[at(t)] * as_column(mid_ref[at(t), :]), axis=1)
+        shifted = (reg_ref[at(t), :] - SHIFTS[step - 1]) * basis[step - 1, at(t), :]
+        return SCALE * (back + shifted)
+
     def operate(step):
-        def project(t, _):
-            column = jnp.sum(voxel[at(t)] * basis[step, at(t), :][:, None, :], axis=2, keepdims=True)
-            z_ref[step, at(t), :] = jnp.sum(jnp.where(eye, column, 0.0), axis=1)
-            my_ref[at(t), :] = jnp.sum(moment_at(t) * column, axis=1)
-            return 0
-
-        lax.fori_loop(0, chunks, project, 0)
         for e in range(2):
             y_send[step, e] = z_ref[step, pl.ds(e * (BY - 1), BX, stride=BY), :]
         for k in range(4):
@@ -293,9 +324,23 @@
             def _():
                 halo_copy(step, k).start()
 
+        def widen(t, _):
+            made = next_basis(step, t)
+            basis[step, at(t), :] = made
+            if step + 1 < ITERS:
+                weighted = reg_ref[at(t), :] * made
+                column = jnp.sum(voxel[at(t)] * weighted[:, None, :], axis=2, keepdims=True)
+                q_ref[at(t), :] = jnp.sum(jnp.where(eye, column, 0.0), axis=1)
+            my_ref[at(t), :] = jnp.sum(block(acc, t) * as_column(z_ref[step, at(t), :]), axis=1)
+            return 0
+
+        lax.fori_loop(0, chunks, widen, 0)
         z = z_ref[step]
         ym_ref[1:bricks, :] = z[: bricks - 1]
         yp_ref[0 : bricks - 1, :] = z[1:]
+        found = []
+        if step + 1 == ITERS:
+            found = [fold(basis[a] * basis[b]) for a, b in early]
         for k in range(4):
 
             @pl.when(here[k])
@@ -310,27 +355,31 @@
         near = near + jnp.where(masks[2], ym_ref[...], 0.0) + jnp.where(masks[3], yp_ref[...], 0.0)
         mid_ref[...] = my_ref[...] + coupling_weight * (degree * z - near)
 
-        def expand(t, _):
-            column = jnp.sum(
-                jnp.where(eye, mid_ref[at(t), :][:, None, :], 0.0), axis=2, keepdims=True
-            )
-            back = jnp.sum(voxel[at(t)] * column, axis=1)
-            shifted = (reg_ref[at(t), :] - SHIFTS[step]) * basis[step, at(t), :]
-            basis[step + 1, at(t), :] = SCALE * (back + shifted)
-            return 0
-
-        lax.fori_loop(0, chunks, expand, 0)
-
-    def fold(values):
-        total = jnp.sum(values, axis=0, keepdims=True)
-        width = total.shape[1]
-        return sum(total[:, c : c + LANES] for c in range(0, width, LANES))
-
+        if step + 1 < ITERS:
+
+            def advance(t, _):
+                back = jnp.sum(block(square, t) * as_column(mid_ref[at(t), :]), axis=1)
+                shifted = q_ref[at(t), :] - SHIFTS[step] * z_ref[step, at(t), :]
+                z_ref[step + 1, at(t), :] = SCALE * (back + shifted)
+                return 0
+
+            lax.fori_loop(0, chunks, advance, 0)
+        else:
+
+            def last(t, _):
+                basis[step + 1, at(t), :] = next_basis(step + 1, t)
+                return 0
+
+            lax.fori_loop(0, chunks, last, 0)
+        return found
+
+    early = [(a, b) for a in range(ITERS) for b in range(a, ITERS)]
+    late = [(a, ITERS) for a in range(ITERS)]
+    pairs = early + late
+    rows = []
     for step in range(ITERS):
-        operate(step)
-
-    pairs = [(a, b) for a in range(ITERS) for b in range(a, ITERS + 1)]
-    rows = [fold(basis[a] * basis[b]) for a, b in pairs]
+        rows = operate(step)
+    rows = rows + [fold(basis[a] * basis[b]) for a, b in late]
     rows = rows + [jnp.zeros_like(rows[0])] * (-len(rows) % 8)
     sums = jnp.sum(jnp.concatenate(rows, axis=0), axis=1, keepdims=True)
     entry = lax.broadcasted_iota(jnp.int32, (len(rows), LANES), 1)
@@ -377,6 +426,7 @@
     res, direction, answer = [one], [one], []
     norm_now = gram[0, 0]
     for step in range(ITERS):
+        before_answer, before_res = answer, res
         image = apply(direction)
         alpha = norm_now / inner(direction, image)
         padded = answer + [jnp.zeros_like(one)] * (len(direction) - len(answer))
@@ -389,12 +439,16 @@
                 p + ratio * d for p, d in zip(res, direction + [jnp.zeros_like(one)])
             ]
             norm_now = norm_next
-    solution_ref[...] = functools.reduce(
-        lambda p, q: p + q, [c * basis[k] for k, c in enumerate(answer)]
-    )
-    residual_ref[...] = functools.reduce(
-        lambda p, q: p + q, [c * basis[k] for k, c in enumerate(res)]
-    )
+    def combine(coefficients):
+        return functools.reduce(
+            lambda p, q: p + q, [c * basis[k] for k, c in enumerate(coefficients)]
+        )
+
+    answer_ref[...] = combine(before_answer)
+    res_ref[...] = combine(before_res)
+    direction_ref[...] = combine(direction)
+    image_ref[...] = combine(image)
+    alpha_ref[...] = jnp.broadcast_to(alpha, alpha_ref.shape)
 
     def drain(j, _):
         to = (me + j * step_by) % count
@@ -421,11 +475,12 @@
     vmem = pl.BlockSpec(memory_space=pltpu.VMEM)
     hbm = pl.BlockSpec(memory_space=pl.ANY)
     f32 = jnp.float32
-    return pl.pallas_call(
+    answer, res, direction, image, alpha = pl.pallas_call(
         functools.partial(kernel, gx, gy),
-        out_shape=(jax.ShapeDtypeStruct((bricks, vox), f32),) * 2,
+        out_shape=(jax.ShapeDtypeStruct((bricks, vox), f32),) * 4
+        + (jax.ShapeDtypeStruct((1, vox), f32),),
         in_specs=[hbm, vmem, vmem, vmem, hbm, vmem],
-        out_specs=(vmem, vmem),
+        out_specs=(vmem,) * 5,
         scratch_shapes=[
             pltpu.VMEM((count, feat, cols), jnp.bfloat16),
             pltpu.VMEM((count, 2 * cols // LANES, LANES), jnp.bfloat16),
@@ -433,8 +488,10 @@
             pltpu.VMEM((count * cols // LANES, LANES), f32),
             pltpu.VMEM((bricks, feat, vox), f32),
             pltpu.VMEM((bricks * feat, LANES), f32),
+            pltpu.VMEM((bricks * feat, LANES), f32),
             pltpu.VMEM((ITERS + 1, bricks, vox), f32),
             pltpu.VMEM((ITERS, bricks, LANES), f32),
+            pltpu.VMEM((bricks, LANES), f32),
             pltpu.VMEM((bricks, LANES), f32),
             pltpu.VMEM((bricks, LANES), f32),
             pltpu.VMEM((bricks, LANES), f32),
@@ -462,6 +519,7 @@
         voxel_feats,
         voxel_reg,
     )
+    return answer + alpha * direction, res - alpha * image
 
 
 def solution(mesh):

time: 48.2 us -> 43.9 us (0.911)
  local copies, waits for them, and re-layouts: 2.95 us -> 0 us
  Pallas kernels: 44.4 us -> 41.5 us
  other arithmetic: 0 us -> 1.6 us
    unnamed x2 -> x0, local copies, waits for them, and re-layouts: 2.95 us -> none
    pallas_call x1, Pallas kernels: 44.4 us -> 41.5 us  [shards(): pl.pallas_call(functools.partial(kernel, gx, gy), out_shape=(jax.ShapeDty...]
    sub x0 -> x1, other arithmetic: none -> 1.6 us  [shards(): return (answer + alpha * direction, res - alpha * image)]
where the time goes in v3:
time: 43.9 us; the launch traced here: 43.7 us
  Pallas kernels  41.5 us (95%)
  other arithmetic  1.6 us (4%)
  between operations  0.64 us (1%)
    pallas_call x1, Pallas kernels, shards(): pl.pallas_call(functools.partial(kernel, gx, gy), out_shape=(jax.ShapeDty...  41.5 us
    sub x1, other arithmetic, shards(): return (answer + alpha * direction, res - alpha * image)  1.6 us

profile of v3, /device:TPU:0, one launch (start us, length us, event | category | flops | bytes accessed | tf_op | source)
XLA Modules:
  0.0 43.7 jit_solution(16172088894175024935)
XLA Ops:
  0.6 41.5 %shard_map.77 = (f32[32,512]{1,0:T(8,128)}, f32[32,512]{1,0:T(8,128)}, f32[32,512]{1,0:T(8,128)}, f32[32,512]{1,0:T(8,128)}, f32[1,512]{1,0:T(1,128)}) custom-call(bf16[32,8192]{1,0:T(8,128)(2,1)} %feats_hbm.1, bf16[64,128]{1,0:T(8,128)(2,1)} %bitcast.5, s32[8,1024]{1,0:T(8,128)} %bitcast.4, s32[4,32]{1,0:T(4,128)} %bitcast.6, f32[32,32,512]{2,1,0:T(8,128)} %voxel_hbm.1, ...), custom_call_target="tpu_custom_call" | custom-call | tf_op jit(solution)/shard_map/pallas_call | solution.py:478
  42.1 1.6 %multiply_subtract_fusion = (f32[32,512]{1,0:T(8,128)}, f32[32,512]{1,0:T(8,128)}) fusion(f32[32,512]{1,0:T(8,128)} %get-tuple-element.10, f32[32,512]{1,0:T(8,128)} %get-tuple-element.11, f32[512]{0:T(512)} %bitcast.7, f32[32,512]{1,0:T(8,128)} %get-tuple-element.7, f32[32,512]{1,0:T(8,128)} %get-tuple-element.9), kind=kLoop, calls=%fused_computation | loop fusion | flops 65536 | bytes 395264 | tf_op jit(solution)/shard_map/sub | solution.py:522

commit v4 on v3

--- a/solution.py
+++ b/solution.py
@@ -236,6 +236,7 @@
         jnp.int32, (1, feat, LANES), 2
     )
     chunks = bricks // CHUNK
+    in_feat = lax.broadcasted_iota(jnp.int32, (bricks, LANES), 1) < feat
 
     def at(t):
         return pl.ds(pl.multiple_of(t * CHUNK, CHUNK), CHUNK)
@@ -254,7 +255,7 @@
         z_ref[0, at(t), :] = jnp.sum(block(square, t) * gathered(t), axis=1)
         return 0
 
-    lax.fori_loop(0, chunks, begin, 0)
+    lax.fori_loop(0, chunks, begin, 0, unroll=True)
 
     linked = jnp.where(adjacency_ref[...] >= 0, 1.0, 0.0)
     same_brick = lax.broadcasted_iota(jnp.int32, (bricks, bricks), 0) == lax.broadcasted_iota(
@@ -341,6 +342,8 @@
         found = []
         if step + 1 == ITERS:
             found = [fold(basis[a] * basis[b]) for a, b in early]
+            final = (reg_ref[...] - SHIFTS[step]) * basis[step]
+            found = found + [fold(basis[a] * final) for a, b in late]
         for k in range(4):
 
             @pl.when(here[k])
@@ -353,7 +356,8 @@
         yp_ref[pl.ds(BY - 1, BX, stride=BY), :] = halo[step, 3]
         near = jnp.where(masks[0], xm, 0.0) + jnp.where(masks[1], xp, 0.0)
         near = near + jnp.where(masks[2], ym_ref[...], 0.0) + jnp.where(masks[3], yp_ref[...], 0.0)
-        mid_ref[...] = my_ref[...] + coupling_weight * (degree * z - near)
+        mid = jnp.where(in_feat, my_ref[...] + coupling_weight * (degree * z - near), 0.0)
+        mid_ref[...] = mid
 
         if step + 1 < ITERS:
 
@@ -363,14 +367,11 @@
                 z_ref[step + 1, at(t), :] = SCALE * (back + shifted)
                 return 0
 
-            lax.fori_loop(0, chunks, advance, 0)
+            lax.fori_loop(0, chunks, advance, 0, unroll=True)
         else:
-
-            def last(t, _):
-                basis[step + 1, at(t), :] = next_basis(step + 1, t)
-                return 0
-
-            lax.fori_loop(0, chunks, last, 0)
+            for e, (a, b) in enumerate(late):
+                e += len(early)
+                found[e] = SCALE * (found[e] + fold(z_ref[a] * mid))
         return found
 
     early = [(a, b) for a in range(ITERS) for b in range(a, ITERS)]
@@ -379,7 +380,6 @@
     rows = []
     for step in range(ITERS):
         rows = operate(step)
-    rows = rows + [fold(basis[a] * basis[b]) for a, b in late]
     rows = rows + [jnp.zeros_like(rows[0])] * (-len(rows) % 8)
     sums = jnp.sum(jnp.concatenate(rows, axis=0), axis=1, keepdims=True)
     entry = lax.broadcasted_iota(jnp.int32, (len(rows), LANES), 1)
@@ -393,6 +393,12 @@
         return 0
 
     lax.fori_loop(1, count, start, 0)
+
+    def last(t, _):
+        basis[ITERS, at(t), :] = next_basis(ITERS, t)
+        return 0
+
+    lax.fori_loop(0, chunks, last, 0)
 
     def finish(j, _):
         source = (me + (count - j) * step_by) % count

time: 43.9 us -> 42.5 us (0.968)
  Pallas kernels: 41.5 us -> 40.1 us
    pallas_call x1, Pallas kernels: 41.5 us -> 40.1 us  [shards(): pl.pallas_call(functools.partial(kernel, gx, gy), out_shape=(jax.ShapeDty...]
where the time goes in v4:
time: 42.5 us; the launch traced here: 42.3 us
  Pallas kernels  40.1 us (94%)
  other arithmetic  1.6 us (4%)
  between operations  0.64 us (2%)
    pallas_call x1, Pallas kernels, shards(): pl.pallas_call(functools.partial(kernel, gx, gy), out_shape=(jax.ShapeDty...  40.1 us
    sub x1, other arithmetic, shards(): return (answer + alpha * direction, res - alpha * image)  1.6 us

profile of v4, /device:TPU:0, one launch (start us, length us, event | category | flops | bytes accessed | tf_op | source)
XLA Modules:
  0.0 42.3 jit_solution(15370237211765673998)
XLA Ops:
  0.6 40.1 %shard_map.77 = (f32[32,512]{1,0:T(8,128)}, f32[32,512]{1,0:T(8,128)}, f32[32,512]{1,0:T(8,128)}, f32[32,512]{1,0:T(8,128)}, f32[1,512]{1,0:T(1,128)}) custom-call(bf16[32,8192]{1,0:T(8,128)(2,1)} %feats_hbm.1, bf16[64,128]{1,0:T(8,128)(2,1)} %bitcast.5, s32[8,1024]{1,0:T(8,128)} %bitcast.4, s32[4,32]{1,0:T(4,128)} %bitcast.6, f32[32,32,512]{2,1,0:T(8,128)} %voxel_hbm.1, ...), custom_call_target="tpu_custom_call" | custom-call | tf_op jit(solution)/shard_map/pallas_call | solution.py:484
  40.7 1.6 %multiply_subtract_fusion = (f32[32,512]{1,0:T(8,128)}, f32[32,512]{1,0:T(8,128)}) fusion(f32[32,512]{1,0:T(8,128)} %get-tuple-element.10, f32[32,512]{1,0:T(8,128)} %get-tuple-element.11, f32[512]{0:T(512)} %bitcast.7, f32[32,512]{1,0:T(8,128)} %get-tuple-element.7, f32[32,512]{1,0:T(8,128)} %get-tuple-element.9), kind=kLoop, calls=%fused_computation | loop fusion | flops 65536 | bytes 395264 | tf_op jit(solution)/shard_map/sub | solution.py:528

commit v5 on v4

--- a/solution.py
+++ b/solution.py
@@ -85,7 +85,7 @@
         )
         return 0
 
-    lax.fori_loop(1, count, greet, 0)
+    lax.fori_loop(1, count, greet, 0, unroll=True)
     voxel_copy = pltpu.make_async_copy(voxel_hbm, voxel, voxel_sem)
     voxel_copy.start()
     halo[...] = jnp.zeros_like(halo)
@@ -392,7 +392,7 @@
         part_copy((me + j * step_by) % count, me).start()
         return 0
 
-    lax.fori_loop(1, count, start, 0)
+    lax.fori_loop(1, count, start, 0, unroll=True)
 
     def last(t, _):
         basis[ITERS, at(t), :] = next_basis(ITERS, t)

time: 42.5 us -> 42.3 us (level)
  no operation moved by 1% of the time
where the time goes in v5:
time: 42.3 us; the launch traced here: 42.1 us
  Pallas kernels  39.8 us (94%)
  other arithmetic  1.6 us (4%)
  between operations  0.64 us (2%)
    pallas_call x1, Pallas kernels, shards(): pl.pallas_call(functools.partial(kernel, gx, gy), out_shape=(jax.ShapeDty...  39.8 us
    sub x1, other arithmetic, shards(): return (answer + alpha * direction, res - alpha * image)  1.6 us

profile of v5, /device:TPU:0, one launch (start us, length us, event | category | flops | bytes accessed | tf_op | source)
XLA Modules:
  0.0 42.1 jit_solution(5193968909324050454)
XLA Ops:
  0.6 39.8 %shard_map.77 = (f32[32,512]{1,0:T(8,128)}, f32[32,512]{1,0:T(8,128)}, f32[32,512]{1,0:T(8,128)}, f32[32,512]{1,0:T(8,128)}, f32[1,512]{1,0:T(1,128)}) custom-call(bf16[32,8192]{1,0:T(8,128)(2,1)} %feats_hbm.1, bf16[64,128]{1,0:T(8,128)(2,1)} %bitcast.5, s32[8,1024]{1,0:T(8,128)} %bitcast.4, s32[4,32]{1,0:T(4,128)} %bitcast.6, f32[32,32,512]{2,1,0:T(8,128)} %voxel_hbm.1, ...), custom_call_target="tpu_custom_call" | custom-call | tf_op jit(solution)/shard_map/pallas_call | solution.py:484
  40.5 1.6 %multiply_subtract_fusion = (f32[32,512]{1,0:T(8,128)}, f32[32,512]{1,0:T(8,128)}) fusion(f32[32,512]{1,0:T(8,128)} %get-tuple-element.10, f32[32,512]{1,0:T(8,128)} %get-tuple-element.11, f32[512]{0:T(512)} %bitcast.7, f32[32,512]{1,0:T(8,128)} %get-tuple-element.7, f32[32,512]{1,0:T(8,128)} %get-tuple-element.9), kind=kLoop, calls=%fused_computation | loop fusion | flops 65536 | bytes 395264 | tf_op jit(solution)/shard_map/sub | solution.py:528
